TPU v7x, 32 devices: a whole 2x2x4 slice. The times are simulated.
32 devices in a mesh: groups: 2 (over y), tok: 4 (over z), slot: 2 (over x), hid: 2 (over core).
Axes of the slice: x: 2, y: 2, z: 4, core: 2. Of those that a mesh axis runs over, the one named last changes fastest.
Arguments:
- tokens: bfloat16 [8192, 1024], P(('groups', 'tok', 'slot', 'hid')), parts along dimension 0, may hold values from -12 to 12
- slot_keys: bfloat16 [2048, 512], P('groups', 'slot'), parts along dimension 0, may hold values from -12 to 12
- w_in: bfloat16 [4, 4, 1024, 4096], P(('groups', 'slot'), 'tok', None, 'hid'), parts along dimension 0, may hold values from -0.1875 to 0.1875
- w_out: bfloat16 [4, 4, 4096, 1024], P(('groups', 'slot'), 'tok', 'hid'), parts along dimension 0, may hold values from -0.09375 to 0.09375
Outputs:
- mixed: float32 [8192, 1024], P(('groups', 'tok', 'slot', 'hid')), parts along dimension 0
There are 2 independent parts, one for each index of `groups`. A program takes and returns all parts, laid end to end along the dimension named above; each array names one. Nothing has to cross between parts.
All inputs are finite; a program needn't handle non-finite values.
Results may differ from a plain program's by a relative error of at most 0.0022.
Values may be sent and summed in bfloat16 or wider, within the bound.
No kernel may reach another device: no remote copies, remote signals or barrier semaphores. Data moves between devices by JAX's collectives and lax.ppermute only.
A program may use at most 64 MiB of HBM per device.

v0:
```python
import jax
import jax.numpy as jnp
from jax import lax
from jax.sharding import PartitionSpec as P

epsilon = 1e-06


def local(tokens, slot_keys, w_in, w_out):
    model_width = tokens.shape[1]
    block_width = slot_keys.shape[1]
    owned_slots = block_width // (lax.axis_size("tok") * lax.axis_size("hid"))
    key_scale = lax.rsqrt(jnp.mean(jnp.square(slot_keys.astype(jnp.float32)), axis=0) + epsilon)
    fragment = lax.all_gather(tokens, "slot", axis=0, tiled=True)
    token_scale = lax.rsqrt(jnp.mean(jnp.square(fragment.astype(jnp.float32)), axis=1) + epsilon)
    logits = (
        4.0
        * token_scale[:, None]
        * key_scale[None, :]
        * jnp.dot(fragment, slot_keys, preferred_element_type=jnp.float32)
        / model_width
    )
    weights_exp = jnp.exp(logits)
    weights_low = weights_exp.astype(jnp.bfloat16)
    slot_numer = lax.dot_general(
        weights_low, fragment, (((0,), (0,)), ((), ())), preferred_element_type=jnp.float32
    )
    slot_denom = jnp.sum(weights_exp, axis=0)
    weights_all = weights_low
    token_denom = jnp.sum(weights_exp, axis=1)
    slot_numer, slot_denom, weights_all, token_denom = (
        slot_numer,
        slot_denom,
        weights_all,
        token_denom,
    )
    summed_numer, summed_denom = lax.psum((slot_numer, slot_denom), ("tok", "hid"))
    first_slot = lax.axis_index(("tok", "hid")) * owned_slots
    owned_numer = lax.dynamic_slice_in_dim(summed_numer, first_slot, owned_slots, 0)
    owned_denom = lax.dynamic_slice_in_dim(summed_denom, first_slot, owned_slots, 0)
    owned_inputs = (owned_numer / owned_denom[:, None]).astype(jnp.bfloat16)
    expert_inputs = lax.all_gather(owned_inputs, "hid", axis=0, tiled=True)
    hidden = jax.nn.gelu(
        jnp.dot(expert_inputs, w_in[0, 0], preferred_element_type=jnp.float32), approximate=True
    ).astype(jnp.bfloat16)
    half_outputs = jnp.dot(hidden, w_out[0, 0], preferred_element_type=jnp.float32)
    owned_outputs = lax.psum_scatter(half_outputs, "hid", scatter_dimension=0, tiled=True).astype(
        jnp.bfloat16
    )
    block_outputs = lax.all_gather(owned_outputs, ("tok", "hid"), axis=0, tiled=True)
    token_numer = jnp.dot(weights_all, block_outputs, preferred_element_type=jnp.float32)
    mine_numer, mine_denom = (
        lax.psum_scatter(token_numer, "slot", scatter_dimension=0, tiled=True),
        lax.psum_scatter(token_denom, "slot", scatter_dimension=0, tiled=True),
    )
    return mine_numer / mine_denom[:, None]


def solution(mesh):
    in_specs = (
        P(("groups", "tok", "slot", "hid"), None),
        P("groups", "slot"),
        P(("groups", "slot"), "tok", None, "hid"),
        P(("groups", "slot"), "tok", "hid", None),
    )
    out_specs = P(("groups", "tok", "slot", "hid"), None)
    return jax.shard_map(local, mesh=mesh, in_specs=in_specs, out_specs=out_specs, check_vma=False)
```

profile of v0, /device:TPU:0, one launch (start us, length us, event | category | flops | bytes accessed | tf_op | source)
XLA Modules:
  0.0 172.2 jit_solution(18349934714928174129)
XLA Ops:
  6.5 0.7 all-gather.2.cloned.1.call-update
  7.3 0.0 all-reduce.3.cloned.1.call-start
  7.3 1.2 multiply_reduce_fusion.1
  8.5 24.4 %all-gather.2.cloned.1.call-done = bf16[512,1024]{1,0:T(8,128)(2,1)} async-done(((bf16[256,1024]{1,0:T(8,128)(2,1)}), bf16[512,1024]{1,0:T(8,128)(2,1)}) %all-gather.2.cloned.1.call-update) | async-done | bytes 1048592 | tf_op jit(solution)/shard_map/all_gather | solution.py:14
  32.9 1.6 multiply_reduce_fusion
  34.5 1.9 %fusion.32 = (f32[512]{0:T(512)S(1)}, f32[256]{0:T(256)S(1)}, bf16[512,256]{1,0:T(8,128)(2,1)S(1)}) fusion(bf16[512,1024]{1,0:T(8,128)(2,1)} %all-gather.2.cloned.1.call-done, bf16[1024,256]{1,0:T(8,128)(2,1)} %param.5, f32[256]{0:T(256)S(1)} %add_rsqrt_fusion, f32[512]{0:T(512)S(1)} %rsqrt_multiply_fusion), kind=kOutput, calls=%fused_computation.34 | convolution fusion | flops 269221120 | bytes 1841152 | tf_op jit(solution)/shard_map/dot_general | solution.py:20
  36.4 1.4 fusion.26
  37.9 0.0 reduce-scatter.3.cloned.1.call-start
  38.0 16.4 %psum.15 = f32[256]{0:T(256)S(1)} all-reduce(f32[256]{0:T(256)S(1)} %get-tuple-element.6), channel_id=1, replica_groups=mesh['groups'=2,'tok'=4,'slot'=2,'hid'=2] {'tok','hid'}, use_global_device_ids=true, to_apply=%region_4.0 | all-reduce | flops 256 | bytes 2048 | tf_op jit(solution)/shard_map/psum | solution.py:37
  54.4 0.1 dynamic_slice.7
  54.5 42.5 %all-reduce.3.cloned.1.call-done = f32[256,1024]{1,0:T(8,128)} async-done(((f32[256,1024]{1,0:T(8,128)}), f32[256,1024]{1,0:T(8,128)}) %all-reduce.3.cloned.1.call-update) | async-done | bytes 1048592 | tf_op jit(solution)/shard_map/psum | solution.py:37
  97.0 1.0 divide_convert_fusion
  98.0 1.9 %all_gather.10 = bf16[64,1024]{1,0:T(8,128)(2,1)S(1)} all-gather(bf16[32,1024]{1,0:T(8,128)(2,1)S(1)} %divide_convert_fusion), channel_id=1, replica_groups=mesh['groups'=2,'tok'=4,'slot'=2,'hid'=2] {'hid'}, dimensions={0}, use_global_device_ids=true | all-gather | bytes 196608 | tf_op jit(solution)/shard_map/all_gather | solution.py:42
  99.9 5.9 %fusion = f32[64,1024]{1,0:T(8,128)} fusion(bf16[1,1,2048,1024]{3,2,1,0:T(8,128)(2,1)} %param.7, bf16[64,1024]{1,0:T(8,128)(2,1)S(1)} %all_gather.10, bf16[1,1,1024,2048]{3,2,1,0:T(8,128)(2,1)} %param.6), kind=kOutput, calls=%fused_computation | convolution fusion | flops 538050560 | bytes 8781824 | tf_op jit(solution)/shard_map/dot_general | solution.py:46
  105.7 0.0 reduce-scatter.5.cloned.1.call-start
  105.8 6.7 %reduce-scatter.3.cloned.1.call-done = f32[32,1024]{1,0:T(8,128)} async-done(((f32[64,1024]{1,0:T(8,128)}), f32[32,1024]{1,0:T(8,128)}) %reduce-scatter.3.cloned.1.call-update) | async-done | bytes 131088 | tf_op jit(solution)/shard_map/reduce_scatter | solution.py:47
  112.5 0.9 convert_element_type.23
  113.4 15.0 %all_gather.11 = bf16[256,1024]{1,0:T(8,128)(2,1)S(1)} all-gather(bf16[32,1024]{1,0:T(8,128)(2,1)S(1)} %convert_element_type.23), channel_id=1, replica_groups=mesh['groups'=2,'tok'=4,'slot'=2,'hid'=2] {'tok','hid'}, dimensions={0}, use_global_device_ids=true | all-gather | bytes 589824 | tf_op jit(solution)/shard_map/all_gather | solution.py:50
  128.4 1.8 %fusion.24 = f32[512,1024]{1,0:T(8,128)} fusion(bf16[256,1024]{1,0:T(8,128)(2,1)S(1)} %all_gather.11, bf16[512,256]{1,0:T(8,128)(2,1)S(1)} %get-tuple-element.7), kind=kOutput, calls=%fused_computation.24 | convolution fusion | flops 268435456 | bytes 2883584 | tf_op jit(solution)/shard_map/dot_general | solution.py:51
  130.3 0.6 dynamic-slice
  131.5 4.9 %all-reduce = f32[512]{0:T(512)S(1)} all-reduce(f32[512]{0:T(512)S(1)} %get-tuple-element.5), channel_id=4, replica_groups=mesh['groups'=2,'tok'=4,'slot'=2,'hid'=2] {'slot'}, use_global_device_ids=true, to_apply=%region_8.0.clone | all-reduce | flops 512 | bytes 4096
  136.4 0.1 dynamic-slice.1
  136.5 26.8 %reduce-scatter.5.cloned.1.call-done = f32[256,1024]{1,0:T(8,128)} async-done(((f32[512,1024]{1,0:T(8,128)}), f32[256,1024]{1,0:T(8,128)}) %reduce-scatter.5.cloned.1.call-update) | async-done | bytes 1048592 | tf_op jit(solution)/shard_map/reduce_scatter | solution.py:53
  163.3 2.3 %broadcast_divide_fusion = f32[256,1024]{1,0:T(8,128)} fusion(f32[256,1024]{1,0:T(8,128)} %reduce-scatter.5.cloned.1.call-done, f32[256]{0:T(256)S(1)} %dynamic-slice.1), kind=kLoop, calls=%fused_computation.18 | loop fusion | flops 262144 | bytes 2098176 | tf_op jit(solution)/shard_map/div | solution.py:56
  (10 shorter events, 0.1 us)
Async XLA Ops:
  6.5 26.4 %all-gather.2.cloned.1.call-start = ((), (), s32[]{:S(2)}) async-start(), calls=%async_computation.2 | async-start | bytes 1572864 | tf_op jit(solution)/shard_map/all_gather | solution.py:14
  7.3 89.7 %all-reduce.3.cloned.1.call-start = ((), (), s32[]{:S(2)}) async-start(), calls=%async_computation.3 | async-start | bytes 2097152 | tf_op jit(solution)/shard_map/psum | solution.py:37
  32.9 3.5 %copy-start = (bf16[512,1024]{1,0:T(8,128)(2,1)S(1)}, bf16[512,1024]{1,0:T(8,128)(2,1)}, u32[]{:S(2)}) copy-start(bf16[512,1024]{1,0:T(8,128)(2,1)} %all-gather.2.cloned.1.call-done) | copy-start | bytes 3145732
  37.9 74.6 %reduce-scatter.3.cloned.1.call-start = ((), (), s32[]{:S(2)}) async-start(), calls=%async_computation.4 | async-start | bytes 393216 | tf_op jit(solution)/shard_map/reduce_scatter | solution.py:47
  105.7 24.5 %copy-start.1 = (u32[32]{0:T(128)S(1)}, u32[32]{0:T(128)}, u32[]{:S(2)}) copy-start(u32[32]{0:T(128)} %constant.43) | copy-start | bytes 388
  105.7 57.6 %reduce-scatter.5.cloned.1.call-start = ((), (), s32[]{:S(2)}) async-start(), calls=%async_computation.5 | async-start | bytes 3145728 | tf_op jit(solution)/shard_map/reduce_scatter | solution.py:53
Sparse Core Ops, SparseCore 0:
  8.9 23.9 all-gather.1
  38.0 58.8 all-reduce.2
  105.9 6.6 reduce-scatter.2
  130.4 32.8 reduce-scatter.4
where the time goes:
time: 173 us; the launch traced here: 172 us
  waiting for transfers between devices  101 us (58%)
  blocking collectives  38.2 us (22%)
  between operations  13.8 us (8%)
  matrix products  11 us (6%)
  other arithmetic  7.06 us (4%)
    psum x1, waiting for transfers between devices, local(): lax.psum((slot_numer, slot_denom), ('tok', 'hid'))  42.5 us
    reduce_scatter x1, waiting for transfers between devices, local(): lax.psum_scatter(token_numer, 'slot', scatter_dimension=0, tiled=True)  26.8 us
    all_gather x1, waiting for transfers between devices, local(): fragment = lax.all_gather(tokens, 'slot', axis=0, tiled=True)  24.4 us
    psum x1, blocking collectives, local(): lax.psum((slot_numer, slot_denom), ('tok', 'hid'))  16.4 us
    all_gather x1, blocking collectives, local(): lax.all_gather(owned_outputs, ('tok', 'hid'), axis=0, tiled=True)  15 us
    reduce_scatter x1, waiting for transfers between devices, local(): lax.psum_scatter(half_outputs, 'hid', scatter_dimension=0, tiled=True)  6.72 us
    dot_general x1, matrix products, local(): jnp.dot(hidden, w_out[0, 0], preferred_element_type=jnp.float32)  5.86 us
    unnamed x1, blocking collectives  4.94 us
  transfers between devices with their start and end apart: 4, of which 4 were waited for; matrix products, arithmetic and copies ran while one was open for 1% of the time, Pallas kernels for 0%

commit v1 on v0

--- a/solution.py
+++ b/solution.py
@@ -34,7 +34,7 @@
         weights_all,
         token_denom,
     )
-    summed_numer, summed_denom = lax.psum((slot_numer, slot_denom), ("tok", "hid"))
+    summed_numer, summed_denom = lax.psum(lax.psum((slot_numer, slot_denom), "hid"), "tok")
     first_slot = lax.axis_index(("tok", "hid")) * owned_slots
     owned_numer = lax.dynamic_slice_in_dim(summed_numer, first_slot, owned_slots, 0)
     owned_denom = lax.dynamic_slice_in_dim(summed_denom, first_slot, owned_slots, 0)

time: 173 us -> 189 us (1.092)
  waiting for transfers between devices: 101 us -> 120 us
  blocking collectives: 38.2 us -> 36.2 us
    psum x1 -> x2, waiting for transfers between devices: 42.5 us -> 60.7 us  [the longest x1 41 us: local(): lax.psum(lax.psum((slot_numer, slot_denom), 'hid'), 'tok')]
    psum x1 -> x2, blocking collectives: 16.4 us -> 14.4 us  [the longest x1 11.9 us: local(): lax.psum(lax.psum((slot_numer, slot_denom), 'hid'), 'tok')]
  transfers between devices with their start and end apart: 4 -> 5, of which waited for: 4 -> 5; matrix products, arithmetic and copies ran while one was open for 1% -> 1% of each run, Pallas kernels for 0% -> 0%
where the time goes in v1:
time: 189 us
  waiting for transfers between devices  120 us (63%)
  blocking collectives  36.2 us (19%)
  between operations  13.8 us (7%)
  matrix products  11 us (6%)
  other arithmetic  7.06 us (4%)
    psum x1, waiting for transfers between devices, local(): lax.psum(lax.psum((slot_numer, slot_denom), 'hid'), 'tok')  41 us
    reduce_scatter x1, waiting for transfers between devices, local(): lax.psum_scatter(token_numer, 'slot', scatter_dimension=0, tiled=True)  26.8 us
    all_gather x1, waiting for transfers between devices, local(): fragment = lax.all_gather(tokens, 'slot', axis=0, tiled=True)  24.4 us
    psum x1, waiting for transfers between devices, local(): lax.psum((slot_numer, slot_denom), 'hid')  19.7 us
    all_gather x1, blocking collectives, local(): lax.all_gather(owned_outputs, ('tok', 'hid'), axis=0, tiled=True)  15 us
    psum x1, blocking collectives, local(): lax.psum(lax.psum((slot_numer, slot_denom), 'hid'), 'tok')  11.9 us
    reduce_scatter x1, waiting for transfers between devices, local(): lax.psum_scatter(half_outputs, 'hid', scatter_dimension=0, tiled=True)  7.14 us
    dot_general x1, matrix products, local(): jnp.dot(hidden, w_out[0, 0], preferred_element_type=jnp.float32)  5.87 us
  transfers between devices with their start and end apart: 5, of which 5 were waited for; matrix products, arithmetic and copies ran while one was open for 1% of the time, Pallas kernels for 0%

profile of v1, /device:TPU:0, one launch (start us, length us, event | category | flops | bytes accessed | tf_op | source)
XLA Modules:
  0.0 188.9 jit_solution(5049426355244155863)
XLA Ops:
  6.5 0.7 all-gather.2.cloned.1.call-update
  7.3 1.2 multiply_reduce_fusion.1
  8.5 24.4 %all-gather.2.cloned.1.call-done = bf16[512,1024]{1,0:T(8,128)(2,1)} async-done(((bf16[256,1024]{1,0:T(8,128)(2,1)}), bf16[512,1024]{1,0:T(8,128)(2,1)}) %all-gather.2.cloned.1.call-update) | async-done | bytes 1048592 | tf_op jit(solution)/shard_map/all_gather | solution.py:14
  32.9 1.6 multiply_reduce_fusion
  34.5 1.9 %fusion.32 = (f32[512]{0:T(512)S(1)}, f32[256]{0:T(256)S(1)}, bf16[512,256]{1,0:T(8,128)(2,1)S(1)}) fusion(bf16[512,1024]{1,0:T(8,128)(2,1)} %all-gather.2.cloned.1.call-done, bf16[1024,256]{1,0:T(8,128)(2,1)} %param.5, f32[256]{0:T(256)S(1)} %add_rsqrt_fusion, f32[512]{0:T(512)S(1)} %rsqrt_multiply_fusion), kind=kOutput, calls=%fused_computation.34 | convolution fusion | flops 269221120 | bytes 1841152 | tf_op jit(solution)/shard_map/dot_general | solution.py:20
  36.4 1.4 fusion.26
  38.0 19.7 %all-reduce.4.cloned.1.call-done = f32[256,1024]{1,0:T(8,128)} async-done(((f32[256,1024]{1,0:T(8,128)}), f32[256,1024]{1,0:T(8,128)}) %all-reduce.4.cloned.1.call-update) | async-done | bytes 1048592 | tf_op jit(solution)/shard_map/psum | solution.py:37
  57.7 2.5 %psum.30 = f32[256]{0:T(256)S(1)} all-reduce(f32[256]{0:T(256)S(1)} %get-tuple-element.6), channel_id=1, replica_groups=mesh['groups'=2,'tok'=4,'slot'=2,'hid'=2] {'hid'}, use_global_device_ids=true, to_apply=%region_5.0 | all-reduce | flops 256 | bytes 2048 | tf_op jit(solution)/shard_map/psum | solution.py:37
  60.2 11.9 %psum.31 = f32[256]{0:T(256)S(1)} all-reduce(f32[256]{0:T(256)S(1)} %psum.30), channel_id=1, replica_groups=mesh['groups'=2,'tok'=4,'slot'=2,'hid'=2] {'tok'}, use_global_device_ids=true, to_apply=%region_6.0 | all-reduce | flops 256 | bytes 2048 | tf_op jit(solution)/shard_map/psum | solution.py:37
  72.2 0.1 dynamic_slice.7
  72.2 41.0 %all-reduce.6.cloned.1.call-done = f32[256,1024]{1,0:T(8,128)} async-done(((f32[256,1024]{1,0:T(8,128)}), f32[256,1024]{1,0:T(8,128)}) %all-reduce.6.cloned.1.call-update) | async-done | bytes 1048592 | tf_op jit(solution)/shard_map/psum | solution.py:37
  113.2 1.0 divide_convert_fusion
  114.2 1.9 %all_gather.10 = bf16[64,1024]{1,0:T(8,128)(2,1)S(1)} all-gather(bf16[32,1024]{1,0:T(8,128)(2,1)S(1)} %divide_convert_fusion), channel_id=1, replica_groups=mesh['groups'=2,'tok'=4,'slot'=2,'hid'=2] {'hid'}, dimensions={0}, use_global_device_ids=true | all-gather | bytes 196608 | tf_op jit(solution)/shard_map/all_gather | solution.py:42
  116.1 5.9 %fusion = f32[64,1024]{1,0:T(8,128)} fusion(bf16[1,1,2048,1024]{3,2,1,0:T(8,128)(2,1)} %param.7, bf16[64,1024]{1,0:T(8,128)(2,1)S(1)} %all_gather.10, bf16[1,1,1024,2048]{3,2,1,0:T(8,128)(2,1)} %param.6), kind=kOutput, calls=%fused_computation | convolution fusion | flops 538050560 | bytes 8781824 | tf_op jit(solution)/shard_map/dot_general | solution.py:46
  122.0 0.0 reduce-scatter.5.cloned.1.call-start
  122.1 7.1 %reduce-scatter.3.cloned.1.call-done = f32[32,1024]{1,0:T(8,128)} async-done(((f32[64,1024]{1,0:T(8,128)}), f32[32,1024]{1,0:T(8,128)}) %reduce-scatter.3.cloned.1.call-update) | async-done | bytes 131088 | tf_op jit(solution)/shard_map/reduce_scatter | solution.py:47
  129.2 0.9 convert_element_type.23
  130.1 15.0 %all_gather.11 = bf16[256,1024]{1,0:T(8,128)(2,1)S(1)} all-gather(bf16[32,1024]{1,0:T(8,128)(2,1)S(1)} %convert_element_type.23), channel_id=1, replica_groups=mesh['groups'=2,'tok'=4,'slot'=2,'hid'=2] {'tok','hid'}, dimensions={0}, use_global_device_ids=true | all-gather | bytes 589824 | tf_op jit(solution)/shard_map/all_gather | solution.py:50
  145.1 1.8 fusion.24
  146.9 0.6 dynamic-slice
  148.2 4.9 %all-reduce = f32[512]{0:T(512)S(1)} all-reduce(f32[512]{0:T(512)S(1)} %get-tuple-element.5), channel_id=4, replica_groups=mesh['groups'=2,'tok'=4,'slot'=2,'hid'=2] {'slot'}, use_global_device_ids=true, to_apply=%region_10.0.clone | all-reduce | flops 512 | bytes 4096
  153.1 0.1 dynamic-slice.1
  153.2 26.8 %reduce-scatter.5.cloned.1.call-done = f32[256,1024]{1,0:T(8,128)} async-done(((f32[512,1024]{1,0:T(8,128)}), f32[256,1024]{1,0:T(8,128)}) %reduce-scatter.5.cloned.1.call-update) | async-done | bytes 1048592 | tf_op jit(solution)/shard_map/reduce_scatter | solution.py:53
  180.0 2.3 %broadcast_divide_fusion = f32[256,1024]{1,0:T(8,128)} fusion(f32[256,1024]{1,0:T(8,128)} %reduce-scatter.5.cloned.1.call-done, f32[256]{0:T(256)S(1)} %dynamic-slice.1), kind=kLoop, calls=%fused_computation.18 | loop fusion | flops 262144 | bytes 2098176 | tf_op jit(solution)/shard_map/div | solution.py:56
  (14 shorter events, 0.2 us)
Async XLA Ops:
  6.5 26.4 %all-gather.2.cloned.1.call-start = ((), (), s32[]{:S(2)}) async-start(), calls=%async_computation.2 | async-start | bytes 1572864 | tf_op jit(solution)/shard_map/all_gather | solution.py:14
  7.3 50.4 %all-reduce.4.cloned.1.call-start = ((), (), s32[]{:S(2)}) async-start(), calls=%async_computation.3 | async-start | bytes 2097152 | tf_op jit(solution)/shard_map/psum | solution.py:37
  32.9 3.5 %copy-start = (bf16[512,1024]{1,0:T(8,128)(2,1)S(1)}, bf16[512,1024]{1,0:T(8,128)(2,1)}, u32[]{:S(2)}) copy-start(bf16[512,1024]{1,0:T(8,128)(2,1)} %all-gather.2.cloned.1.call-done) | copy-start | bytes 3145732
  37.9 75.3 %all-reduce.6.cloned.1.call-start = ((), (), s32[]{:S(2)}) async-start(), calls=%async_computation.4 | async-start | bytes 2097152 | tf_op jit(solution)/shard_map/psum | solution.py:37
  57.7 71.5 %reduce-scatter.3.cloned.1.call-start = ((), (), s32[]{:S(2)}) async-start(), calls=%async_computation.5 | async-start | bytes 393216 | tf_op jit(solution)/shard_map/reduce_scatter | solution.py:47
  122.0 24.9 %copy-start.1 = (u32[32]{0:T(128)S(1)}, u32[32]{0:T(128)}, u32[]{:S(2)}) copy-start(u32[32]{0:T(128)} %constant.43) | copy-start | bytes 388
  122.0 58.0 %reduce-scatter.5.cloned.1.call-start = ((), (), s32[]{:S(2)}) async-start(), calls=%async_computation.6 | async-start | bytes 3145728 | tf_op jit(solution)/shard_map/reduce_scatter | solution.py:53
Sparse Core Ops, SparseCore 0:
  8.9 23.9 all-gather.1
  38.0 19.5 all-reduce.3
  60.2 53.0 all-reduce.5
  122.1 7.0 reduce-scatter.2
  147.1 32.9 reduce-scatter.4
